TPU v7x, 32 devices: a whole 2x2x4 slice. The times are simulated.
32 devices in a mesh: groups: 2 (over x), space: 16 (over z, y, core).
Axes of the slice: x: 2, y: 2, z: 4, core: 2. Of those that a mesh axis runs over, the one named last changes fastest.
Arguments:
- lifted_field: float32 [64, 16, 128, 256], P('groups', 'space'), parts along dimension 0, may hold values from -6 to 6
- cotangent: bfloat16 [64, 16, 128, 256], P('groups', 'space'), parts along dimension 0, may hold values from -6 to 6
- spectral_weights: float32 [2, 32, 1024, 32, 32], P(None, None, 'space'), may hold values from -4 to 4
- point_weights: float32 [32, 32], replicated, may hold values from -1 to 1
- point_bias: float32 [32], replicated, may hold values from -3 to 3
Outputs:
- activated: bfloat16 [64, 16, 128, 256], P('groups', 'space'), parts along dimension 0
- grad_spectral: float32 [4, 32, 1024, 32, 32], P('groups', None, 'space'), parts along dimension 0
- grad_point: float32 [64, 32], P('groups'), parts along dimension 0
- grad_bias: float32 [64], P('groups'), parts along dimension 0
There are 2 independent parts, one for each index of `groups`. A program takes and returns all parts, laid end to end along the dimension named above; an argument that names none is the same for every part. Nothing has to cross between parts.
All inputs are finite; a program needn't handle non-finite values.
Results may differ from a plain program's by a relative error of at most 0.001.
Values sent between devices are 32-bit elements; how exact they have to be, the bound alone decides.
A program may use at most 192 MiB of HBM per device.

v0:
```python
import functools

import jax
import jax.numpy as jnp
import numpy as np
from jax import lax
from jax.experimental import pallas as pl
from jax.experimental.pallas import tpu as pltpu
from jax.sharding import PartitionSpec as P

MX = 32
MY = 32
MZ = 32
ROWS = 8
STEP = 32

HIGH = lax.Precision.HIGH
INV_SQRT_TWO = 0.7071067811865476
INV_SQRT_TWO_PI = 0.3989422804014327


def angles(positions, frequency, length):
    product = np.outer(np.asarray(positions), np.asarray(frequency)) % length
    phase = 2.0 * np.pi / length * product.astype(np.float64)
    return np.cos(phase), np.sin(phase)


def kept(count, length):
    index = np.arange(count)
    return np.where(index < count // 2, index, length - count + index)


def halves(table):
    table = np.asarray(table, np.float32)
    high = table.astype(jnp.bfloat16)
    low = (table - high.astype(np.float32)).astype(jnp.bfloat16)
    return jnp.asarray(high), jnp.asarray(low)


def split(value):
    high = value.astype(jnp.bfloat16)
    low = (value - high.astype(jnp.float32)).astype(jnp.bfloat16)
    return high, low


def dot3(a, b, dims=(((1,), (0,)), ((), ()))):
    one = functools.partial(
        lax.dot_general, dimension_numbers=dims, preferred_element_type=jnp.float32
    )
    return one(a[0], b[0]) + (one(a[0], b[1]) + one(a[1], b[0]))


def forward_tables(ny, nz):
    cos_z, sin_z = angles(np.arange(nz), np.arange(MZ), nz)
    table_z = np.concatenate([cos_z, -sin_z, -sin_z, -cos_z], axis=1)
    cos_y, sin_y = angles(np.arange(ny), kept(MY, ny), ny)
    table_y = np.concatenate([cos_y.T, sin_y.T], axis=0)
    return halves(table_z) + halves(table_y)


def inverse_tables(ny, nz, scale, local_rows):
    cos_z, sin_z = angles(np.arange(nz), np.arange(MZ), nz)
    weight = np.where(np.arange(MZ) == 0, 1.0, 2.0)[:, None] * scale
    real = np.kron(np.eye(4), cos_z.T * weight)
    imag = np.kron(np.eye(4), -sin_z.T * weight)
    cos_y, sin_y = angles(np.arange(ny), kept(MY, ny), ny)
    cos_y = cos_y.reshape(ny, MY // local_rows, local_rows)
    sin_y = sin_y.reshape(ny, MY // local_rows, local_rows)
    real_y = np.stack([cos_y, -sin_y], 2).reshape(ny, 2 * MY)
    imag_y = np.stack([sin_y, cos_y], 2).reshape(ny, 2 * MY)
    return halves(np.concatenate([real, imag], 0)) + halves(np.concatenate([real_y, imag_y], 0))


def finish_y(lines, ty, modes_ref):
    def one(c, carry):
        both = dot3(ty, split(lines[c]))
        turned = pltpu.roll(both[MY:], 2 * MZ, 1)
        modes_ref[c] = (both[:MY] + turned)[:, : 2 * MZ]
        return carry

    lax.fori_loop(0, lines.shape[0], one, 0, unroll=16)


def forward_kernel(x_ref, tzh, tzl, tyh, tyl, modes_ref, lines):
    step = pl.program_id(1)
    channels, rows, nz = x_ref.shape
    value = x_ref[...].reshape(channels * rows, nz)
    along = dot3(split(value), (tzh[...], tzl[...]))
    start = pl.multiple_of(step * rows, rows)
    lines[:, pl.ds(start, rows), :] = along.reshape(channels, rows, 4 * MZ)

    @pl.when(step == pl.num_programs(1) - 1)
    def _():
        finish_y(lines, (tyh[...], tyl[...]), modes_ref)


def whole(array):
    shape = array.shape
    return pl.BlockSpec(shape, lambda *_: (0,) * len(shape))


def field_spec(channels, nz):
    return pl.BlockSpec((channels, None, STEP, nz), lambda x, y: (0, x, y, 0))


def modes_spec(channels):
    return pl.BlockSpec((None, channels, MY, 2 * MZ), lambda x, y: (x, 0, 0, 0))


def forward_modes(field):
    channels, width, ny, nz = field.shape
    tables = forward_tables(ny, nz)
    return pl.pallas_call(
        forward_kernel,
        grid=(width, ny // STEP),
        out_shape=jax.ShapeDtypeStruct((width, channels, MY, 2 * MZ), jnp.float32),
        in_specs=[field_spec(channels, nz)] + [whole(t) for t in tables],
        out_specs=modes_spec(channels),
        scratch_shapes=[pltpu.VMEM((channels, ny, 4 * MZ), jnp.float32)],
        name="forward_modes",
    )(field, *tables)


def middle_kernel(
    m_ref, x_ref, cot_ref, w_ref, bias_ref, pick, bdh, bdl, iyh, iyl, tzh, tzl, tyh, tyl,
    act_ref, modes_ref, point_ref, lines, inverse, field_part, wh, wl, total,
):
    step = pl.program_id(1)
    channels, rows, nz = x_ref.shape
    quads = channels // 4
    width = 4 * MZ
    ny = lines.shape[1]

    def same_row():
        size = channels * ROWS
        row = lax.broadcasted_iota(jnp.int32, (size, size), 0) % ROWS
        column = lax.broadcasted_iota(jnp.int32, (size, size), 1) % ROWS
        return row == column

    @pl.when(step == 0)
    def _():
        for part in range(0, m_ref.shape[1], 256):
            lanes = pl.ds(part, 256)
            both = dot3((iyh[...], iyl[...]), split(m_ref[:, lanes]))
            inverse[0, :, lanes] = both[:ny]
            inverse[1, :, lanes] = both[ny:]
        contract = (((1,), (1,)), ((), ()))
        for narrow, out in zip(split(w_ref[...]), (wh, wl)):
            tall = lax.dot_general(
                pick[...], narrow, contract, preferred_element_type=jnp.float32
            ).astype(jnp.bfloat16)
            square = lax.dot_general(tall, pick[...], contract, preferred_element_type=jnp.float32)
            out[...] = jnp.where(same_row(), square, 0.0).astype(jnp.bfloat16)
        total[...] = jnp.zeros_like(total)

    first = pl.multiple_of(step * rows, rows)
    stacked = jnp.concatenate(
        [
            jnp.concatenate(
                [
                    inverse[r, pl.ds(first, rows), g * width : (g + 1) * width]
                    for r in range(2)
                ],
                axis=1,
            )
            for g in range(quads)
        ],
        axis=0,
    )
    stacked = split(stacked)
    for c in range(4):
        lanes = slice(c * nz, (c + 1) * nz)
        field_part[:, lanes] = dot3(stacked, (bdh[:, lanes], bdl[:, lanes]))

    for half in range(rows // ROWS):
        here = slice(half * ROWS, (half + 1) * ROWS)
        start = pl.multiple_of(step * rows + half * ROWS, ROWS)
        spectral = jnp.concatenate(
            [
                field_part[
                    g * rows + half * ROWS : g * rows + (half + 1) * ROWS, c * nz : (c + 1) * nz
                ]
                for g in range(quads)
                for c in range(4)
            ],
            axis=0,
        )
        field = split(x_ref[:, here, :].reshape(channels * ROWS, nz))
        before = spectral + dot3((wh[...], wl[...]), field)
        before = before.reshape(channels, ROWS, nz) + bias_ref[...]
        normal = 0.5 * (1.0 + lax.erf(before * INV_SQRT_TWO))
        density = jnp.exp(-0.5 * before * before) * INV_SQRT_TWO_PI
        act_ref[:, here, :] = (before * normal).astype(jnp.bfloat16)
        slope = cot_ref[:, here, :].astype(jnp.float32) * (normal + before * density)
        slope = split(slope.reshape(channels * ROWS, nz))
        total[...] += dot3(field, slope, (((1,), (1,)), ((), ())))
        along = dot3(slope, (tzh[...], tzl[...]))
        lines[:, pl.ds(start, ROWS), :] = along.reshape(channels, ROWS, 4 * MZ)

    @pl.when(step == pl.num_programs(1) - 1)
    def _():
        finish_y(lines, (tyh[...], tyl[...]), modes_ref)
        size = channels * ROWS
        diagonal = jnp.where(same_row(), total[...], 0.0)
        point_ref[...] = jnp.sum(diagonal.reshape(channels, ROWS, size), axis=1)


def middle(grid_modes, local_rows, field, cotangent, point_weights, point_bias, scale):
    channels, width, ny, nz = field.shape
    size = channels * ROWS
    tables = inverse_tables(ny, nz, scale, local_rows) + forward_tables(ny, nz)
    pick = jnp.asarray(np.repeat(np.eye(channels, dtype=np.float32), ROWS, 0).astype(jnp.bfloat16))
    bias = jnp.broadcast_to(point_bias[:, None, None], (channels, 1, nz))
    spec = field_spec(channels, nz)
    mixed_spec = pl.BlockSpec((None,) + grid_modes.shape[1:], lambda x, y: (x, 0, 0))
    return pl.pallas_call(
        middle_kernel,
        grid=(width, ny // STEP),
        out_shape=(
            jax.ShapeDtypeStruct(field.shape, jnp.bfloat16),
            jax.ShapeDtypeStruct((width, channels, MY, 2 * MZ), jnp.float32),
            jax.ShapeDtypeStruct((width, channels, size), jnp.float32),
        ),
        in_specs=[mixed_spec, spec, spec, whole(point_weights), whole(bias), whole(pick)]
        + [whole(t) for t in tables],
        out_specs=(
            spec,
            modes_spec(channels),
            pl.BlockSpec((None, channels, size), lambda x, y: (x, 0, 0)),
        ),
        scratch_shapes=[
            pltpu.VMEM((channels, ny, 4 * MZ), jnp.float32),
            pltpu.VMEM((2, ny, channels * MZ), jnp.float32),
            pltpu.VMEM((channels // 4 * STEP, 4 * nz), jnp.float32),
            pltpu.VMEM((size, size), jnp.bfloat16),
            pltpu.VMEM((size, size), jnp.bfloat16),
            pltpu.VMEM((size, size), jnp.float32),
        ],
        name="middle",
    )(grid_modes, field, cotangent, point_weights, bias, pick, *tables)


def weight_gradient(spectrum, slope_modes):
    turned = jnp.stack([slope_modes[1], -slope_modes[0]], axis=0)
    slope_modes, turned = lax.optimization_barrier((slope_modes, turned))
    real = spectrum[0][None, :, :, None, :]
    imag = spectrum[1][None, :, :, None, :]
    out = real * slope_modes[:, :, None] + imag * turned[:, :, None]
    return out.transpose(0, 1, 4, 2, 3)


def x_table(length_x):
    return angles(np.arange(length_x), kept(MX, length_x), length_x)


def exchange_kernel(devices, src, out, send_sem, recv_sem, own_sem):
    me = lax.axis_index("space")
    barrier = pltpu.get_barrier_semaphore()

    def greet(step, carry):
        peer = lax.rem(me + step, devices)
        pl.semaphore_signal(
            barrier, inc=1, device_id={"space": peer}, device_id_type=pl.DeviceIdType.MESH
        )
        return carry

    def copy(step, slot):
        peer = lax.rem(me + step, devices)
        return pltpu.make_async_remote_copy(
            src_ref=src.at[peer],
            dst_ref=out.at[slot],
            send_sem=send_sem.at[step],
            recv_sem=recv_sem.at[step],
            device_id={"space": peer},
            device_id_type=pl.DeviceIdType.MESH,
        )

    def send(step, carry):
        copy(step, me).start()
        return carry

    def finish(step, carry):
        done = copy(step, lax.rem(me + devices - step, devices))
        done.wait_send()
        done.wait_recv()
        return carry

    lax.fori_loop(1, devices, greet, 0)
    own = pltpu.make_async_copy(src.at[me], out.at[me], own_sem)
    own.start()
    pl.semaphore_wait(barrier, devices - 1)
    lax.fori_loop(1, devices, send, 0)
    own.wait()
    lax.fori_loop(1, devices, finish, 0)


def exchange(lines, identity):
    devices = lax.axis_size("space")
    shape = lines.shape
    lines = lines.reshape(devices, -1, 128)
    vmem = pl.BlockSpec(memory_space=pltpu.VMEM)
    out = pl.pallas_call(
        functools.partial(exchange_kernel, devices),
        out_shape=jax.ShapeDtypeStruct(lines.shape, jnp.float32),
        in_specs=[vmem],
        out_specs=vmem,
        scratch_shapes=[
            pltpu.SemaphoreType.DMA((devices,)),
            pltpu.SemaphoreType.DMA((devices,)),
            pltpu.SemaphoreType.DMA,
        ],
        compiler_params=pltpu.CompilerParams(collective_id=identity, has_side_effects=True),
        name=f"exchange_{identity}",
    )(lines)
    return out.reshape(shape)


def to_spectrum(modes, scale, devices, extra=None):
    width, channels = modes.shape[:2]
    local = MY * MZ // devices
    lines = modes.reshape(width, channels, MY, 2, MZ).transpose(0, 3, 1, 2, 4)
    lines = lines.reshape(width, 2, channels, devices, local).transpose(3, 0, 1, 2, 4)
    lines = lines.reshape(devices, width * 2 * channels * local)
    size = lines.shape[1]
    if extra is not None:
        extra = jnp.pad(extra, (0, -extra.shape[0] % 128))
        extra = jnp.broadcast_to(extra[None], (devices,) + extra.shape)
        lines = jnp.concatenate([lines, extra], axis=1)
    lines = exchange(lines, 0 if extra is None else 2)
    summed = jnp.sum(lines[:, size:], axis=0)
    lines = lines[:, :size].reshape(devices * width, 2, channels, local)
    cos_x, sin_x = x_table(devices * width)
    table = np.stack([np.stack([cos_x, -sin_x], 1), np.stack([sin_x, cos_x], 1)], 1)
    table = jnp.asarray((table * scale).astype(np.float32))
    return jnp.einsum("xrcm,xrqk->qkcm", lines, table, precision=HIGH), summed


def mix_modes(spectrum, weights):
    real, imag = spectrum[0], spectrum[1]
    out_real = jnp.einsum("kim,kmio->kom", real, weights[0], precision=HIGH) - jnp.einsum(
        "kim,kmio->kom", imag, weights[1], precision=HIGH
    )
    out_imag = jnp.einsum("kim,kmio->kom", real, weights[1], precision=HIGH) + jnp.einsum(
        "kim,kmio->kom", imag, weights[0], precision=HIGH
    )
    return jnp.stack([out_real, out_imag], axis=0)


def to_grid(mixed, length_x):
    channels = mixed.shape[2]
    cos_x, sin_x = x_table(length_x)
    table = np.stack([np.stack([cos_x, sin_x], 0), np.stack([-sin_x, cos_x], 0)], 0)
    table = jnp.asarray(table.astype(np.float32))
    lines = jnp.einsum("rkom,rqxk->xqom", mixed, table, precision=HIGH)
    local = mixed.shape[3]
    devices = MY * MZ // local
    width = length_x // devices
    if local % MZ == 0:
        local_rows = local // MZ
        lines = lines.reshape(length_x, 2, channels, local_rows, MZ).transpose(0, 1, 3, 2, 4)
        lines = exchange(lines.reshape(length_x, 2 * local_rows * channels * MZ), 1)
        grid = lines.reshape(devices, width, 2 * local_rows, channels * MZ).transpose(1, 0, 2, 3)
    else:
        local_rows = 1
        lines = exchange(lines.reshape(length_x, 2 * channels * local), 1)
        grid = lines.reshape(MY, MZ // local, width, 2, channels, local).transpose(2, 0, 3, 4, 1, 5)
    return grid.reshape(width, 2 * MY, channels * MZ), local_rows


def body(lifted_field, cotangent, spectral_weights, point_weights, point_bias):
    devices = lax.axis_size("space")
    channels, width, ny, nz = lifted_field.shape
    length_x = width * devices
    scale = 1.0 / float(length_x * ny * nz) ** 0.5
    spectrum, _ = to_spectrum(forward_modes(lifted_field), scale, devices)
    grid_modes, local_rows = to_grid(mix_modes(spectrum, spectral_weights), length_x)
    activated, slope_modes, wide_point = middle(
        grid_modes, local_rows, lifted_field, cotangent, point_weights, point_bias, scale
    )
    local_point = jnp.sum(wide_point.reshape(width, channels, channels, ROWS), axis=(0, 3))
    local_bias = jnp.sum(slope_modes[:, :, 0, 0], axis=0)
    partial = jnp.concatenate([local_point.reshape(-1), local_bias])
    slope_spectrum, summed = to_spectrum(slope_modes, scale, devices, partial)
    area = channels * channels
    summed_point = summed[:area].reshape(channels, channels)
    summed_bias = summed[area : area + channels]
    local_modes = spectrum.shape[3]
    mode_ids = lax.axis_index("space") * local_modes + jnp.arange(local_modes, dtype=jnp.int32)
    weight_modes = jnp.where(mode_ids % MZ == 0, 1.0, 2.0).astype(jnp.float32)
    grad_spectral = weight_gradient(spectrum, slope_spectrum * weight_modes)
    return (activated, grad_spectral, summed_point * scale, summed_bias * scale)


def solution(mesh):
    placed = (
        P("groups", "space", None, None),
        P("groups", "space", None, None),
        P(None, None, "space", None, None),
        P(),
        P(),
    )
    return jax.shard_map(
        body,
        mesh=mesh,
        in_specs=placed,
        out_specs=(
            P("groups", "space", None, None),
            P("groups", None, "space", None, None),
            P("groups", None),
            P("groups"),
        ),
        check_vma=False,
    )
```

profile of v0, /device:TPU:0, one launch (start us, length us, event | category | flops | bytes accessed | tf_op | source)
XLA Modules:
  0.0 112.3 jit_solution(2982345556036741848)
XLA Ops:
  0.7 1.4 %broadcast_in_dim.12.bias_ref = f32[32,1,256]{2,1,0:T(1,128)} broadcast(f32[32]{0:T(128)} %param.25), dimensions={0} | broadcast | bytes 32896 | tf_op jit(solution)/shard_map/broadcast_in_dim | solution.py:213
  2.0 6.4 %forward_modes.1 = f32[1,32,32,64]{3,2,1,0:T(8,128)} custom-call(f32[32,1,128,256]{3,2,1,0:T(8,128)} %x_ref.3, bf16[256,128]{1,0:T(8,128)(2,1)} %constant.55.clone.tzh, bf16[256,128]{1,0:T(8,128)(2,1)} %constant.56.clone.tzl, bf16[64,128]{1,0:T(8,128)(2,1)} %constant.57.clone.tyh, bf16[64,128]{1,0:T(8,128)(2,1)} %constant.58.clone.tyl), custom_call_target="tpu_custom_call" | custom-call | tf_op jit(solution)/shard_map/forward_modes/pallas_call | solution.py:113
  8.4 1.6 %reshape.80 = f32[1,32,32,2,32]{4,3,2,1,0:T(2,128)S(1)} reshape(f32[1,32,32,64]{3,2,1,0:T(8,128)} %forward_modes.1) | data formatting | bytes 524288 | tf_op jit(solution)/shard_map/reshape | solution.py:321
  10.0 0.1 copy.140
  10.2 0.2 reshape.81
  10.4 0.2 copy.67
  10.6 0.8 reshape_reshape.9.src
  11.4 12.7 %exchange_0.1 = f32[16,32,128]{2,1,0:T(8,128)} custom-call(f32[16,32,128]{2,1,0:T(8,128)} %reshape_reshape.9.src), custom_call_target="tpu_custom_call" | custom-call | tf_op jit(solution)/shard_map/exchange_0/pallas_call | solution.py:302
  24.2 1.1 reshape_reshape.10
  25.3 1.6 %convolution_bitcast_fusion.1 = f32[2,32,32,64]{3,1,2,0:T(8,128)S(1)} fusion(f32[16,2,2,32,1]{3,0,1,4,2:T(8,128)} %constant.74, f32[16,2,32,64]{3,2,1,0:T(8,128)S(1)} %reshape_reshape.10), kind=kOutput, calls=%fused_computation.10 | convolution fusion | flops 25165824 | bytes 794624 | tf_op jit(solution)/shard_map/xrcm,xrqk->qkcm/dot_general | solution.py:335
  26.9 0.1 slice_bitcast_fusion
  26.9 0.3 copy.116
  27.2 0.3 copy.115
  27.6 0.0 copy-start.1
  27.6 13.5 %fusion.2 = (f32[32,64,32]{1,2,0:T(8,128)S(1)}, f32[32,64,32]{1,2,0:T(8,128)S(1)}, f32[32,64,32]{1,2,0:T(8,128)S(1)}, f32[32,64,32]{1,2,0:T(8,128)S(1)}) fusion(f32[2,32,64,32,32]{2,4,3,1,0:T(8,128)} %param.23, f32[32,64,32]{1,2,0:T(8,128)S(1)} %copy.115, f32[32,64,32]{1,2,0:T(8,128)S(1)} %copy.116), kind=kLoop, calls=%fused_computation.7 | loop fusion | flops 16515072 | bytes 18350080
  41.1 0.0 copy-start
  41.1 1.2 %fusion.10 = (f32[1,32,32,64]{3,1,0,2:T(8,128)S(1)}, f32[1,32,32,64]{3,1,0,2:T(8,128)S(1)}) fusion(f32[32,64,32]{1,2,0:T(8,128)S(1)} %get-tuple-element.18, f32[32,64,32]{1,2,0:T(8,128)S(1)} %get-tuple-element.15, f32[32,64,32]{1,2,0:T(8,128)S(1)} %get-tuple-element.19, f32[32,64,32]{1,2,0:T(8,128)S(1)} %get-tuple-element.14), kind=kLoop, calls=%fused_computation.27 | loop fusion | flops 131072 | bytes 1572864 | tf_op jit(solution)/shard_map/stack | solution.py:346
  42.2 0.0 copy-done.1
  42.2 0.4 convolution_bitcast_fusion.2
  42.7 0.6 reshape.82
  43.3 0.6 copy.139
  43.9 1.0 reshape_reshape.11.src
  44.9 12.2 %exchange_1.1 = f32[16,32,128]{2,1,0:T(8,128)} custom-call(f32[16,32,128]{2,1,0:T(8,128)} %reshape_reshape.11.src), custom_call_target="tpu_custom_call" | custom-call | tf_op jit(solution)/shard_map/exchange_1/pallas_call | solution.py:302
  57.1 1.7 %reshape_transpose_reshape_reshape.3.m_ref = f32[1,64,1024]{2,1,0:T(8,128)} reshape(f32[16,32,128]{2,1,0:T(8,128)} %exchange_1.1) | data formatting | bytes 524288 | tf_op jit(solution)/shard_map/reshape;transpose;reshape;reshape | solution.py:367
  58.8 18.1 %middle.1 = (bf16[32,1,128,256]{3,2,1,0:T(8,128)(2,1)}, f32[1,32,32,64]{3,2,1,0:T(8,128)}, f32[1,32,256]{2,1,0:T(8,128)}) custom-call(f32[1,64,1024]{2,1,0:T(8,128)} %reshape_transpose_reshape_reshape.3.m_ref, f32[32,1,128,256]{3,2,1,0:T(8,128)} %x_ref.3, bf16[32,1,128,256]{3,2,1,0:T(8,128)(2,1)} %cot_ref.1, f32[32,32]{1,0:T(8,128)} %w_ref.1, ...), custom_call_target="tpu_custom_call" | custom-call | tf_op jit(solution)/shard_map/middle/pallas_call | solution.py:216
  76.8 1.2 %slice_reduce_fusion.1 = f32[32]{0:T(128)S(1)} fusion(f32[1,32,32,64]{3,2,1,0:T(8,128)} %get-tuple-element.10), kind=kLoop, calls=%fused_computation.35 | loop fusion | bytes 256 | tf_op jit(solution)/shard_map/slice | solution.py:381
  78.1 0.9 copy.73
  79.0 0.1 copy.74
  79.0 0.1 reshape.87
  79.1 1.7 %reshape.83 = f32[1,32,32,2,32]{4,3,2,1,0:T(2,128)S(1)} reshape(f32[1,32,32,64]{3,2,1,0:T(8,128)} %get-tuple-element.10) | data formatting | bytes 524288 | tf_op jit(solution)/shard_map/reshape | solution.py:321
  80.8 0.1 copy.138
  80.9 0.2 reshape.84
  81.2 0.2 copy.72
  81.3 0.2 reshape.85
  81.6 0.8 reshape.88.src
  82.4 13.5 %exchange_2.1 = f32[16,41,128]{2,1,0:T(8,128)} custom-call(f32[16,41,128]{2,1,0:T(8,128)} %reshape.88.src), custom_call_target="tpu_custom_call" | custom-call | tf_op jit(solution)/shard_map/exchange_2/pallas_call | solution.py:302
  95.8 1.1 copy.141
  97.0 0.5 slice_multiply_fusion.1
  97.5 0.7 mul.81
  98.2 0.2 reshape.90
  98.4 0.0 copy-done
  98.4 0.8 fusion.5
  99.2 0.1 fusion.15
  99.3 0.1 pad_maximum_fusion
  99.5 0.6 copy.76
  100.1 0.6 copy.78
  100.7 11.6 %multiply_add_fusion = f32[2,32,64,32,32]{2,4,3,1,0:T(8,128)} fusion(f32[2,32,64,32]{2,3,1,0:T(8,128)S(1)} %copy.78, f32[32,64,32]{1,2,0:T(8,128)S(1)} %copy.116, f32[2,32,64,32]{2,3,1,0:T(8,128)S(1)} %copy.76, f32[32,64,32]{1,2,0:T(8,128)S(1)} %copy.115), kind=kLoop, calls=%fused_computation | loop fusion | flops 12582912 | bytes 18350080 | tf_op jit(solution)/shard_map/add | solution.py:248
  (8 shorter events, 0.1 us)
Async XLA Ops:
  27.6 14.7 %copy-start.1 = (f32[2,2,16,32,1]{3,2,0,1,4:T(8,128)S(1)}, f32[2,2,16,32,1]{3,2,0,1,4:T(8,128)}, u32[]{:S(2)}) copy-start(f32[2,2,16,32,1]{3,2,0,1,4:T(8,128)} %constant.75) | copy-start | bytes 24580
  41.1 57.3 %copy-start = (f32[16,2,2,32,1]{3,0,1,2,4:T(8,128)S(1)}, f32[16,2,2,32,1]{3,0,1,2,4:T(8,128)}, u32[]{:S(2)}) copy-start(f32[16,2,2,32,1]{3,0,1,2,4:T(8,128)} %constant.76) | copy-start | bytes 24580
where the time goes:
time: 113 us; the launch traced here: 112 us
  Pallas kernels  62.8 us (56%)
  other arithmetic  27.1 us (24%)
  local copies, waits for them, and re-layouts  18.7 us (17%)
  matrix products  2.83 us (3%)
    pallas_call x3, Pallas kernels, exchange(): pl.pallas_call(functools.partial(exchange_kernel, devices), out_shape=jax...  38.4 us
    pallas_call x1, Pallas kernels, middle(): pl.pallas_call(middle_kernel, grid=(width, ny // STEP), out_shape=(jax.Sh...  18.1 us
    unnamed x1, other arithmetic  13.5 us
    add x1, other arithmetic, weight_gradient(): out = real * slope_modes[:, :, None] + imag * turned[:, :, None]  11.6 us
    pallas_call x1, Pallas kernels, forward_modes(): pl.pallas_call(forward_kernel, grid=(width, ny // STEP), out_shape=jax.Sh...  6.38 us
    reshape x4, local copies, waits for them, and re-layouts, to_spectrum(): lines = modes.reshape(width, channels, MY, 2, MZ).transpose(0, 3, 1, 2, 4)  3.56 us
    dot_general x2, matrix products, to_spectrum(): return (jnp.einsum('xrcm,xrqk->qkcm', lines, table, precision=HIGH), summed)  2.4 us

commit v1 on v0

--- a/solution.py
+++ b/solution.py
@@ -64,10 +64,16 @@
     real = np.kron(np.eye(4), cos_z.T * weight)
     imag = np.kron(np.eye(4), -sin_z.T * weight)
     cos_y, sin_y = angles(np.arange(ny), kept(MY, ny), ny)
-    cos_y = cos_y.reshape(ny, MY // local_rows, local_rows)
-    sin_y = sin_y.reshape(ny, MY // local_rows, local_rows)
-    real_y = np.stack([cos_y, -sin_y], 2).reshape(ny, 2 * MY)
-    imag_y = np.stack([sin_y, cos_y], 2).reshape(ny, 2 * MY)
+    if local_rows is None:
+        cos_y = np.concatenate([cos_y[:, 0::2], cos_y[:, 1::2]], axis=1)
+        sin_y = np.concatenate([sin_y[:, 0::2], sin_y[:, 1::2]], axis=1)
+        real_y = np.concatenate([cos_y, -sin_y], axis=1)
+        imag_y = np.concatenate([sin_y, cos_y], axis=1)
+    else:
+        cos_y = cos_y.reshape(ny, MY // local_rows, local_rows)
+        sin_y = sin_y.reshape(ny, MY // local_rows, local_rows)
+        real_y = np.stack([cos_y, -sin_y], 2).reshape(ny, 2 * MY)
+        imag_y = np.stack([sin_y, cos_y], 2).reshape(ny, 2 * MY)
     return halves(np.concatenate([real, imag], 0)) + halves(np.concatenate([real_y, imag_y], 0))
 
 
@@ -249,6 +255,271 @@
     return out.transpose(0, 1, 4, 2, 3)
 
 
+def packed_tables(ny, nz):
+    cos_z, sin_z = angles(np.arange(nz), np.arange(MZ), nz)
+    table_z = np.concatenate([cos_z, cos_z, -sin_z, -sin_z], axis=1)
+    cos_y, sin_y = angles(np.arange(ny), kept(MY, ny), ny)
+    cos_y, sin_y = cos_y.T, sin_y.T
+    table_y = np.concatenate([cos_y[0::2], cos_y[1::2], sin_y[0::2], sin_y[1::2]], axis=0)
+    return halves(table_z) + halves(table_y)
+
+
+def lane_ids(rows):
+    return lax.broadcasted_iota(jnp.int32, (rows, 4 * MZ), 1)
+
+
+def turn(value):
+    rolled = pltpu.roll(value, 2 * MZ, 1)
+    return jnp.where(lane_ids(value.shape[0]) < 2 * MZ, rolled, -rolled)
+
+
+def message_rows(ty, line):
+    both = dot3(ty, split(line))
+    count = MY // 2
+    even = lane_ids(count) // MZ % 2 == 0
+    cos_part = jnp.where(even, both[:count], both[count : 2 * count])
+    sin_part = jnp.where(even, both[2 * count : 3 * count], both[3 * count :])
+    return cos_part + turn(sin_part)
+
+
+def along_x(parts, sign):
+    length = len(parts)
+    half = length // 2
+    plus = [parts[x] + parts[length - x] for x in range(1, half)]
+    minus = [turn(parts[x] - parts[length - x]) for x in range(1, half)]
+    ends = (parts[0] + parts[half], parts[0] - parts[half])
+    out = [None] * length
+    for k in range(half + 1):
+        even = ends[k % 2]
+        odd = None
+        for x in range(1, half):
+            even = even + plus[x - 1] * float(np.cos(2 * np.pi * (k * x % length) / length))
+            if 0 < k < half:
+                term = minus[x - 1] * float(np.sin(2 * np.pi * (k * x % length) / length))
+                odd = term if odd is None else odd + term
+        if odd is None:
+            out[k] = even
+        else:
+            out[k] = even + odd if sign > 0 else even - odd
+            out[length - k] = even - odd if sign > 0 else even + odd
+    return out
+
+
+def greet_peers(devices):
+    me = lax.axis_index("space")
+    barrier = pltpu.get_barrier_semaphore()
+
+    def greet(step, carry):
+        pl.semaphore_signal(
+            barrier,
+            inc=1,
+            device_id={"space": lax.rem(me + step, devices)},
+            device_id_type=pl.DeviceIdType.MESH,
+        )
+        return carry
+
+    lax.fori_loop(1, devices, greet, 0)
+
+
+def meet_peers(devices):
+    pl.semaphore_wait(pltpu.get_barrier_semaphore(), devices - 1)
+
+
+def message(devices, channels, src, recv, sems, step, part, owner):
+    me = lax.axis_index("space")
+    peer = lax.rem(me + step, devices)
+    there = pl.ds(pl.multiple_of(peer * channels + part * 8, 8), 8)
+    here = pl.ds(pl.multiple_of(owner * channels + part * 8, 8), 8)
+    return pltpu.make_async_remote_copy(
+        src_ref=src.at[there],
+        dst_ref=recv.at[here],
+        send_sem=sems.at[0, part, step],
+        recv_sem=sems.at[1, part, step],
+        device_id={"space": peer},
+        device_id_type=pl.DeviceIdType.MESH,
+    )
+
+
+def send_part(devices, channels, src, recv, sems, part):
+    me = lax.axis_index("space")
+
+    def send(step, carry):
+        message(devices, channels, src, recv, sems, step, part, me).start()
+        return carry
+
+    lax.fori_loop(1, devices, send, 0)
+
+
+def keep_own(channels, src, recv):
+    me = lax.axis_index("space")
+    own = pl.ds(pl.multiple_of(me * channels, channels), channels)
+    recv[own, :] = src[own, :]
+
+
+def take_part(devices, channels, src, recv, sems, part):
+    me = lax.axis_index("space")
+
+    def take(step, carry):
+        owner = lax.rem(me + devices - step, devices)
+        done = message(devices, channels, src, recv, sems, step, part, owner)
+        done.wait_send()
+        done.wait_recv()
+        return carry
+
+    lax.fori_loop(1, devices, take, 0)
+
+
+def x_modes(devices, channels, scale, recv, part, real_ref, imag_ref):
+    start = pl.multiple_of(part * 8, 8)
+    parts = [recv[pl.ds(x * channels + start, 8), :] for x in range(devices)]
+    for k, value in enumerate(along_x(parts, 1)):
+        value = value * scale
+        real, imag = value[:, : 2 * MZ], value[:, 2 * MZ :]
+        for alias in range(k, real_ref.shape[0], devices):
+            real_ref[alias, pl.ds(start, 8), :] = real
+            imag_ref[alias, pl.ds(start, 8), :] = imag
+
+
+def front_kernel(
+    devices, channels, scale, x_ref, tzh, tzl, tyh, tyl, real_ref, imag_ref, lines, src, recv, sems
+):
+    part = pl.program_id(0)
+
+    @pl.when(part == 0)
+    def _():
+        greet_peers(devices)
+
+    rows, ny, nz = x_ref.shape
+    value = x_ref[...].reshape(rows * ny, nz)
+    along = dot3(split(value), (tzh[...], tzl[...]))
+    lines[...] = along.reshape(rows, ny, 4 * MZ)
+    ty = (tyh[...], tyl[...])
+    for c in range(rows):
+        src[pl.ds(part * rows + c, devices, stride=channels), :] = message_rows(ty, lines[c])
+
+    @pl.when(part == 0)
+    def _():
+        meet_peers(devices)
+
+    send_part(devices, channels, src, recv, sems, part)
+
+    @pl.when(part == pl.num_programs(0) - 1)
+    def _():
+        keep_own(channels, src, recv)
+
+        def finish(part, carry):
+            take_part(devices, channels, src, recv, sems, part)
+            x_modes(devices, channels, scale, recv, part, real_ref, imag_ref)
+            return carry
+
+        lax.fori_loop(0, channels // 8, finish, 0)
+
+
+def front(field, devices, scale):
+    channels, _, ny, nz = field.shape
+    tables = packed_tables(ny, nz)
+    parts = channels // 8
+    spectrum = jax.ShapeDtypeStruct((MX, channels, 2 * MZ), jnp.float32)
+    return pl.pallas_call(
+        functools.partial(front_kernel, devices, channels, scale),
+        grid=(parts,),
+        out_shape=(spectrum, spectrum),
+        in_specs=[pl.BlockSpec((8, None, ny, nz), lambda c: (c, 0, 0, 0))]
+        + [whole(t) for t in tables],
+        out_specs=(whole(spectrum), whole(spectrum)),
+        scratch_shapes=[
+            pltpu.VMEM((8, ny, 4 * MZ), jnp.float32),
+            pltpu.VMEM((devices * channels, 4 * MZ), jnp.float32),
+            pltpu.VMEM((devices * channels, 4 * MZ), jnp.float32),
+            pltpu.SemaphoreType.DMA((2, parts, devices)),
+        ],
+        compiler_params=pltpu.CompilerParams(
+            collective_id=0, has_side_effects=True, vmem_limit_bytes=14 * 2**20
+        ),
+        cost_estimate=pl.CostEstimate(flops=10**10, bytes_accessed=40 * 10**6, transcendentals=0),
+        name="front",
+    )(field, *tables)
+
+
+def mix_kernel(devices, channels, real_ref, imag_ref, w_ref, out_ref, mixed, src, recv, sems):
+    greet_peers(devices)
+    local = real_ref.shape[2]
+    aliases = range(0, real_ref.shape[0], devices)
+    parts = channels // 8
+
+    def one_part(part, carry):
+        start = pl.multiple_of(part * 8, 8)
+        rows = pl.ds(start, 8)
+
+        def one_k(k, inner):
+            out_real = jnp.zeros((8, local), jnp.float32)
+            out_imag = jnp.zeros((8, local), jnp.float32)
+            for i in range(channels):
+                real = jnp.broadcast_to(real_ref[k, i : i + 1, :], (8, local))
+                imag = jnp.broadcast_to(imag_ref[k, i : i + 1, :], (8, local))
+                w_real = w_ref[0, k, i, rows, :]
+                w_imag = w_ref[1, k, i, rows, :]
+                for alias in aliases[1:]:
+                    w_real = w_real + w_ref[0, k + alias, i, rows, :]
+                    w_imag = w_imag + w_ref[1, k + alias, i, rows, :]
+                out_real = out_real + (real * w_real - imag * w_imag)
+                out_imag = out_imag + (real * w_imag + imag * w_real)
+            mixed[k] = jnp.concatenate([out_real, out_imag], axis=1)
+            return inner
+
+        lax.fori_loop(0, devices, one_k, 0)
+        for x, value in enumerate(along_x([mixed[k] for k in range(devices)], -1)):
+            src[pl.ds(x * channels + start, 8), :] = value
+
+        @pl.when(part == 0)
+        def _():
+            meet_peers(devices)
+
+        send_part(devices, channels, src, recv, sems, part)
+        return carry
+
+    lax.fori_loop(0, parts, one_part, 0)
+    keep_own(channels, src, recv)
+
+    def finish(part, carry):
+        take_part(devices, channels, src, recv, sems, part)
+        return carry
+
+    lax.fori_loop(0, parts, finish, 0)
+    for quad in range(channels // 4):
+        rows = [
+            recv[pl.ds(quad * 4 + c, devices, stride=channels), :] for c in range(4)
+        ]
+        for block in range(4):
+            lanes = slice(block * MZ, (block + 1) * MZ)
+            out_ref[
+                block * devices : (block + 1) * devices, quad * 4 * MZ : (quad + 1) * 4 * MZ
+            ] = jnp.concatenate([row[:, lanes] for row in rows], axis=1)
+
+
+def mix_to_grid(real, imag, weights, devices):
+    channels = real.shape[1]
+    weights = pltpu.with_memory_space_constraint(weights.transpose(0, 1, 3, 4, 2), pltpu.VMEM)
+    out = jax.ShapeDtypeStruct((4 * devices, channels * MZ), jnp.float32)
+    vmem = pl.BlockSpec(memory_space=pltpu.VMEM)
+    return pl.pallas_call(
+        functools.partial(mix_kernel, devices, channels),
+        out_shape=out,
+        in_specs=[vmem, vmem, vmem],
+        out_specs=vmem,
+        scratch_shapes=[
+            pltpu.VMEM((devices, 8, 4 * MZ), jnp.float32),
+            pltpu.VMEM((devices * channels, 4 * MZ), jnp.float32),
+            pltpu.VMEM((devices * channels, 4 * MZ), jnp.float32),
+            pltpu.SemaphoreType.DMA((2, channels // 8, devices)),
+        ],
+        compiler_params=pltpu.CompilerParams(
+            collective_id=1, has_side_effects=True, vmem_limit_bytes=8 * 2**20
+        ),
+        name="mix",
+    )(real, imag, weights)
+
+
 def x_table(length_x):
     return angles(np.arange(length_x), kept(MX, length_x), length_x)
 
@@ -372,8 +643,15 @@
     channels, width, ny, nz = lifted_field.shape
     length_x = width * devices
     scale = 1.0 / float(length_x * ny * nz) ** 0.5
-    spectrum, _ = to_spectrum(forward_modes(lifted_field), scale, devices)
-    grid_modes, local_rows = to_grid(mix_modes(spectrum, spectral_weights), length_x)
+    packed = width == 1 and MY == 2 * devices and MX % devices == 0 and channels % 8 == 0
+    if packed:
+        real, imag = front(lifted_field, devices, scale)
+        grid_modes = mix_to_grid(real, imag, spectral_weights, devices)[None]
+        local_rows = None
+        spectrum = jnp.stack([real, imag], axis=0)
+    else:
+        spectrum, _ = to_spectrum(forward_modes(lifted_field), scale, devices)
+        grid_modes, local_rows = to_grid(mix_modes(spectrum, spectral_weights), length_x)
     activated, slope_modes, wide_point = middle(
         grid_modes, local_rows, lifted_field, cotangent, point_weights, point_bias, scale
     )

time: 113 us -> 102 us (0.903)
  other arithmetic: 27.1 us -> 12.5 us
  local copies, waits for them, and re-layouts: 18.7 us -> 26.5 us
  Pallas kernels: 62.8 us -> 60.7 us
  matrix products: 2.83 us -> 0.83 us
    pallas_call x3 -> x1, Pallas kernels: 38.4 us -> 11 us  [exchange(): pl.pallas_call(functools.partial(exchange_kernel, devices), out_shape=jax...]
    pallas_call x1 -> x2, Pallas kernels: 6.38 us -> 31.8 us  [the longest x1 17.4 us: mix_to_grid(): pl.pallas_call(functools.partial(mix_kernel, devices, channels), out_shap...]
    unnamed x8 -> x17, local copies, waits for them, and re-layouts: 1.8 us -> 17.6 us
    unnamed x1 -> x0, other arithmetic: 13.5 us -> none
    another operation x4 -> x0, local copies, waits for them, and re-layouts: 4.6 us -> none  [the longest x2 1.82 us: exchange(): lines = lines.reshape(devices, -1, 128)]
    reshape x4 -> x2, local copies, waits for them, and re-layouts: 3.56 us -> 1.78 us  [to_spectrum(): lines = modes.reshape(width, channels, MY, 2, MZ).transpose(0, 3, 1, 2, 4)]
    dot_general x2 -> x1, matrix products: 2.4 us -> 0.83 us  [to_spectrum(): return (jnp.einsum('xrcm,xrqk->qkcm', lines, table, precision=HIGH), summed)]
    reshape x2 -> x0, local copies, waits for them, and re-layouts: 1.22 us -> none  [to_grid(): lines.reshape(length_x, 2, channels, local_rows, MZ)]
where the time goes in v1:
time: 102 us; the launch traced here: 101 us
  Pallas kernels  60.7 us (60%)
  local copies, waits for them, and re-layouts  26.5 us (26%)
  other arithmetic  12.5 us (12%)
    pallas_call x1, Pallas kernels, middle(): pl.pallas_call(middle_kernel, grid=(width, ny // STEP), out_shape=(jax.Sh...  17.9 us
    unnamed x17, local copies, waits for them, and re-layouts  17.6 us
    pallas_call x1, Pallas kernels, mix_to_grid(): pl.pallas_call(functools.partial(mix_kernel, devices, channels), out_shap...  17.4 us
    pallas_call x1, Pallas kernels, front(): pl.pallas_call(functools.partial(front_kernel, devices, channels, scale),...  14.3 us
    add x1, other arithmetic, weight_gradient(): out = real * slope_modes[:, :, None] + imag * turned[:, :, None]  11.6 us
    pallas_call x1, Pallas kernels, exchange(): pl.pallas_call(functools.partial(exchange_kernel, devices), out_shape=jax...  11 us

profile of v1, /device:TPU:0, one launch (start us, length us, event | category | flops | bytes accessed | tf_op | source)
XLA Modules:
  0.0 101.3 jit_solution(1874948726214378544)
XLA Ops:
  0.7 1.4 %broadcast_in_dim.15.bias_ref = f32[32,1,256]{2,1,0:T(1,128)} broadcast(f32[32]{0:T(128)} %param.23), dimensions={0} | broadcast | bytes 32896 | tf_op jit(solution)/shard_map/broadcast_in_dim | solution.py:219
  2.0 0.0 copy-start.1
  2.0 2.2 %copy-done.1 = f32[32,1,128,256]{3,2,1,0:T(8,128)S(1)} copy-done((f32[32,1,128,256]{3,2,1,0:T(8,128)S(1)}, f32[32,1,128,256]{3,2,1,0:T(8,128)}, u32[]{:S(2)}) %copy-start.1) | copy-done | bytes 4194328
  4.2 0.0 copy-start.3
  4.2 0.8 copy-done.3
  5.1 0.0 copy-start.4
  5.1 0.8 copy-done.4
  5.9 0.0 copy-start.5
  5.9 0.7 copy-done.5
  6.6 0.0 copy-start.6
  6.6 0.7 copy-done.6
  7.3 0.0 copy-start.7
  7.3 14.3 %front.1 = (f32[32,32,64]{2,1,0:T(8,128)S(1)}, f32[32,32,64]{2,1,0:T(8,128)S(1)}) custom-call(f32[32,1,128,256]{3,2,1,0:T(8,128)S(1)} %copy-done.1, bf16[256,128]{1,0:T(8,128)(2,1)S(1)} %copy-done.4, bf16[256,128]{1,0:T(8,128)(2,1)S(1)} %copy-done.3, bf16[64,128]{1,0:T(8,128)(2,1)S(1)} %copy-done.6, bf16[64,128]{1,0:T(8,128)(2,1)S(1)} %copy-done.5), custom_call_target="tpu_custom_call" | custom-call | flops 10000000000 | bytes 40000000 | tf_op jit(solution)/shard_map/front/pallas_call | solution.py:423
  21.7 0.0 copy-start
  21.7 10.5 %copy-done = f32[2,32,64,32,32]{2,4,3,1,0:T(8,128)S(1)} copy-done((f32[2,32,64,32,32]{2,4,3,1,0:T(8,128)S(1)}, f32[2,32,64,32,32]{2,4,3,1,0:T(8,128)}, u32[]{:S(2)}) %copy-start) | copy-done | bytes 16777240
  32.2 17.4 %mix.1 = f32[64,1024]{1,0:T(8,128)S(1)} custom-call(f32[32,32,64]{2,1,0:T(8,128)S(1)} %get-tuple-element.11.real_ref, f32[32,32,64]{2,1,0:T(8,128)S(1)} %get-tuple-element.12.imag_ref, f32[2,32,32,32,64]{4,3,2,1,0:T(8,128)S(1)} %bitcast.36), custom_call_target="tpu_custom_call" | custom-call | tf_op jit(solution)/shard_map/mix/pallas_call | solution.py:505
  49.7 0.0 copy-start.2
  49.7 0.7 copy-done.2
  50.4 17.9 %middle.1 = (bf16[32,1,128,256]{3,2,1,0:T(8,128)(2,1)}, f32[1,32,32,64]{3,2,1,0:T(8,128)}, f32[1,32,256]{2,1,0:T(8,128)}) custom-call(f32[1,64,1024]{2,1,0:T(8,128)} %bitcast.39, f32[32,1,128,256]{3,2,1,0:T(8,128)} %x_ref.3, bf16[32,1,128,256]{3,2,1,0:T(8,128)(2,1)} %cot_ref.1, f32[32,32]{1,0:T(8,128)} %w_ref.1, f32[32,1,256]{2,1,0:T(1,128)} %broadcast_in_dim.15.bias_ref, ...), custom_call_target="tpu_custom_call" | custom-call | tf_op jit(solution)/shard_map/middle/pallas_call | solution.py:222
  68.3 1.2 %slice_reduce_fusion.1 = f32[32]{0:T(128)S(1)} fusion(f32[1,32,32,64]{3,2,1,0:T(8,128)} %get-tuple-element.14), kind=kLoop, calls=%fused_computation.12 | loop fusion | bytes 256 | tf_op jit(solution)/shard_map/slice | solution.py:659
  69.5 0.9 copy.44
  70.4 0.1 copy.45
  70.5 0.1 reshape.75
  70.6 1.7 %reshape.71 = f32[1,32,32,2,32]{4,3,2,1,0:T(2,128)S(1)} reshape(f32[1,32,32,64]{3,2,1,0:T(8,128)} %get-tuple-element.14) | data formatting | bytes 524288 | tf_op jit(solution)/shard_map/reshape | solution.py:592
  72.2 0.1 copy.58
  72.4 0.2 reshape.72
  72.6 0.2 copy.43
  72.8 0.2 reshape.73
  73.0 0.8 reshape.76.src
  73.8 11.0 %exchange_2.1 = f32[16,41,128]{2,1,0:T(8,128)} custom-call(f32[16,41,128]{2,1,0:T(8,128)} %reshape.76.src), custom_call_target="tpu_custom_call" | custom-call | tf_op jit(solution)/shard_map/exchange_2/pallas_call | solution.py:573
  84.8 1.1 %copy.59 = f32[2,8,41,128]{3,1,2,0:T(8,128)S(1)} copy(f32[2,8,41,128]{3,2,1,0:T(8,128)} %bitcast.45) | data formatting | bytes 671744
  86.0 0.5 slice_multiply_fusion.1
  86.5 0.7 mul.81
  87.2 0.2 reshape.78
  87.4 0.0 copy-done.7
  87.4 0.8 fusion.1
  88.2 0.1 fusion.4
  88.4 0.1 pad_maximum_fusion
  88.5 0.6 copy.47
  89.1 0.6 copy.48
  89.7 11.6 %multiply_add_fusion = f32[2,32,64,32,32]{2,4,3,1,0:T(8,128)} fusion(f32[2,32,64,32]{2,3,1,0:T(8,128)S(1)} %copy.48, f32[32,64,32]{1,2,0:T(8,128)S(1)} %bitcast.38, f32[2,32,64,32]{2,3,1,0:T(8,128)S(1)} %copy.47, f32[32,64,32]{1,2,0:T(8,128)S(1)} %bitcast.37), kind=kLoop, calls=%fused_computation | loop fusion | flops 12582912 | bytes 18350080 | tf_op jit(solution)/shard_map/add | solution.py:254
  (8 shorter events, 0.1 us)
Async XLA Ops:
  2.0 2.2 %copy-start.1 = (f32[32,1,128,256]{3,2,1,0:T(8,128)S(1)}, f32[32,1,128,256]{3,2,1,0:T(8,128)}, u32[]{:S(2)}) copy-start(f32[32,1,128,256]{3,2,1,0:T(8,128)} %x_ref.3) | copy-start | bytes 12582916
  4.2 0.8 copy-start.3
  5.1 0.8 copy-start.4
  5.9 0.7 copy-start.5
  6.6 0.7 copy-start.6
  7.3 80.1 %copy-start.7 = (f32[16,2,2,32,1]{3,0,1,2,4:T(8,128)S(1)}, f32[16,2,2,32,1]{3,0,1,2,4:T(8,128)}, u32[]{:S(2)}) copy-start(f32[16,2,2,32,1]{3,0,1,2,4:T(8,128)} %constant.79) | copy-start | bytes 24580
  21.7 10.5 %copy-start = (f32[2,32,64,32,32]{2,4,3,1,0:T(8,128)S(1)}, f32[2,32,64,32,32]{2,4,3,1,0:T(8,128)}, u32[]{:S(2)}) copy-start(f32[2,32,64,32,32]{2,4,3,1,0:T(8,128)} %param.21) | copy-start | bytes 50331652
  49.7 0.7 copy-start.2

commit v2 on v1

--- a/solution.py
+++ b/solution.py
@@ -434,9 +434,8 @@
             pltpu.SemaphoreType.DMA((2, parts, devices)),
         ],
         compiler_params=pltpu.CompilerParams(
-            collective_id=0, has_side_effects=True, vmem_limit_bytes=14 * 2**20
+            collective_id=0, has_side_effects=True
         ),
-        cost_estimate=pl.CostEstimate(flops=10**10, bytes_accessed=40 * 10**6, transcendentals=0),
         name="front",
     )(field, *tables)
 
@@ -447,34 +446,31 @@
     aliases = range(0, real_ref.shape[0], devices)
     parts = channels // 8
 
-    def one_part(part, carry):
-        start = pl.multiple_of(part * 8, 8)
-        rows = pl.ds(start, 8)
-
-        def one_k(k, inner):
-            out_real = jnp.zeros((8, local), jnp.float32)
-            out_imag = jnp.zeros((8, local), jnp.float32)
-            for i in range(channels):
-                real = jnp.broadcast_to(real_ref[k, i : i + 1, :], (8, local))
-                imag = jnp.broadcast_to(imag_ref[k, i : i + 1, :], (8, local))
+    def one_k(k, carry):
+        totals = [jnp.zeros((8, local), jnp.float32)] * (2 * parts)
+        for i in range(channels):
+            real = jnp.broadcast_to(real_ref[k, i : i + 1, :], (8, local))
+            imag = jnp.broadcast_to(imag_ref[k, i : i + 1, :], (8, local))
+            for part in range(parts):
+                rows = slice(part * 8, part * 8 + 8)
                 w_real = w_ref[0, k, i, rows, :]
                 w_imag = w_ref[1, k, i, rows, :]
                 for alias in aliases[1:]:
                     w_real = w_real + w_ref[0, k + alias, i, rows, :]
                     w_imag = w_imag + w_ref[1, k + alias, i, rows, :]
-                out_real = out_real + (real * w_real - imag * w_imag)
-                out_imag = out_imag + (real * w_imag + imag * w_real)
-            mixed[k] = jnp.concatenate([out_real, out_imag], axis=1)
-            return inner
-
-        lax.fori_loop(0, devices, one_k, 0)
-        for x, value in enumerate(along_x([mixed[k] for k in range(devices)], -1)):
+                totals[2 * part] = totals[2 * part] + (real * w_real - imag * w_imag)
+                totals[2 * part + 1] = totals[2 * part + 1] + (real * w_imag + imag * w_real)
+        for part in range(parts):
+            mixed[k, part] = jnp.concatenate(totals[2 * part : 2 * part + 2], axis=1)
+        return carry
+
+    lax.fori_loop(0, devices, one_k, 0)
+    meet_peers(devices)
+
+    def one_part(part, carry):
+        start = pl.multiple_of(part * 8, 8)
+        for x, value in enumerate(along_x([mixed[k, part] for k in range(devices)], -1)):
             src[pl.ds(x * channels + start, 8), :] = value
-
-        @pl.when(part == 0)
-        def _():
-            meet_peers(devices)
-
         send_part(devices, channels, src, recv, sems, part)
         return carry
 
@@ -508,7 +504,7 @@
         in_specs=[vmem, vmem, vmem],
         out_specs=vmem,
         scratch_shapes=[
-            pltpu.VMEM((devices, 8, 4 * MZ), jnp.float32),
+            pltpu.VMEM((devices, channels // 8, 8, 4 * MZ), jnp.float32),
             pltpu.VMEM((devices * channels, 4 * MZ), jnp.float32),
             pltpu.VMEM((devices * channels, 4 * MZ), jnp.float32),
             pltpu.SemaphoreType.DMA((2, channels // 8, devices)),
@@ -518,6 +514,262 @@
         ),
         name="mix",
     )(real, imag, weights)
+
+
+def middle_packed_kernel(
+    devices, m_ref, x_ref, cot_ref, w_ref, bias_ref, pick, bdh, bdl, iyh, iyl, tzh, tzl, tyh, tyl,
+    act_ref, modes_ref, point_ref, lines, inverse, field_part, wh, wl, total, bias, point,
+):
+    step = pl.program_id(1)
+    channels, rows, nz = x_ref.shape
+    quads = channels // 4
+    width = 4 * MZ
+    ny = lines.shape[1]
+
+    def same_row():
+        size = channels * ROWS
+        row = lax.broadcasted_iota(jnp.int32, (size, size), 0) % ROWS
+        column = lax.broadcasted_iota(jnp.int32, (size, size), 1) % ROWS
+        return row == column
+
+    @pl.when(step == 0)
+    def _():
+        for part in range(0, m_ref.shape[1], 256):
+            lanes = pl.ds(part, 256)
+            both = dot3((iyh[...], iyl[...]), split(m_ref[:, lanes]))
+            inverse[0, :, lanes] = both[:ny]
+            inverse[1, :, lanes] = both[ny:]
+        contract = (((1,), (1,)), ((), ()))
+        for narrow, out in zip(split(w_ref[...]), (wh, wl)):
+            tall = lax.dot_general(
+                pick[...], narrow, contract, preferred_element_type=jnp.float32
+            ).astype(jnp.bfloat16)
+            square = lax.dot_general(tall, pick[...], contract, preferred_element_type=jnp.float32)
+            out[...] = jnp.where(same_row(), square, 0.0).astype(jnp.bfloat16)
+        total[...] = jnp.zeros_like(total)
+        rest = jnp.broadcast_to(bias_ref[...], (nz, channels))
+        wide = jnp.zeros_like(bias)
+        for _ in range(3):
+            narrow = rest.astype(jnp.bfloat16)
+            rest = rest - narrow.astype(jnp.float32)
+            wide = wide + lax.dot_general(
+                pick[...], narrow, contract, preferred_element_type=jnp.float32
+            )
+        bias[...] = wide
+
+    first = pl.multiple_of(step * rows, rows)
+    stacked = jnp.concatenate(
+        [
+            jnp.concatenate(
+                [
+                    inverse[r, pl.ds(first, rows), g * width : (g + 1) * width]
+                    for r in range(2)
+                ],
+                axis=1,
+            )
+            for g in range(quads)
+        ],
+        axis=0,
+    )
+    stacked = split(stacked)
+    for c in range(4):
+        lanes = slice(c * nz, (c + 1) * nz)
+        field_part[:, lanes] = dot3(stacked, (bdh[:, lanes], bdl[:, lanes]))
+
+    for half in range(rows // ROWS):
+        here = slice(half * ROWS, (half + 1) * ROWS)
+        start = pl.multiple_of(step * rows + half * ROWS, ROWS)
+        spectral = jnp.concatenate(
+            [
+                field_part[
+                    g * rows + half * ROWS : g * rows + (half + 1) * ROWS, c * nz : (c + 1) * nz
+                ]
+                for g in range(quads)
+                for c in range(4)
+            ],
+            axis=0,
+        )
+        field = split(x_ref[:, here, :].reshape(channels * ROWS, nz))
+        before = spectral + dot3((wh[...], wl[...]), field)
+        before = (before + bias[...]).reshape(channels, ROWS, nz)
+        normal = 0.5 * (1.0 + lax.erf(before * INV_SQRT_TWO))
+        density = jnp.exp(-0.5 * before * before) * INV_SQRT_TWO_PI
+        act_ref[:, here, :] = (before * normal).astype(jnp.bfloat16)
+        slope = cot_ref[:, here, :].astype(jnp.float32) * (normal + before * density)
+        slope = split(slope.reshape(channels * ROWS, nz))
+        total[...] += dot3(field, slope, (((1,), (1,)), ((), ())))
+        along = dot3(slope, (tzh[...], tzl[...]))
+        lines[:, pl.ds(start, ROWS), :] = along.reshape(channels, ROWS, 4 * MZ)
+
+    @pl.when(step == pl.num_programs(1) - 1)
+    def _():
+        ty = (tyh[...], tyl[...])
+
+        def finish(c, carry):
+            modes_ref[pl.ds(c, devices, stride=channels), :] = message_rows(ty, lines[c])
+            return carry
+
+        lax.fori_loop(0, channels, finish, 0, unroll=8)
+        diagonal = jnp.where(same_row(), total[...], 0.0)
+        rows_sum = jnp.sum(diagonal.reshape(channels, ROWS, channels * ROWS), axis=1)
+        high, low = split(rows_sum)
+        folded = jnp.dot(high, pick[...], preferred_element_type=jnp.float32) + jnp.dot(
+            low, pick[...], preferred_element_type=jnp.float32
+        )
+        own_bias = modes_ref[:channels, :channels]
+        lane = lax.broadcasted_iota(jnp.int32, (channels, channels), 1)
+        own_bias = jnp.where(lane == 0, own_bias, 0.0)
+        spare = jnp.zeros((channels, 4 * MZ - 2 * channels), jnp.float32)
+        point[...] = jnp.concatenate([folded, own_bias, spare], axis=1)
+        first_rows = point[pl.ds(0, channels // 2, stride=2), :]
+        second_rows = point[pl.ds(1, channels // 2, stride=2), :]
+        packed = first_rows + pltpu.roll(second_rows, 2 * MZ, 1)
+        for d in range(channels // 2):
+            point_ref[d] = packed[d : d + 1]
+
+
+def middle_packed(grid_modes, devices, field, cotangent, point_weights, point_bias, scale):
+    channels, width, ny, nz = field.shape
+    size = channels * ROWS
+    tables = inverse_tables(ny, nz, scale, None) + packed_tables(ny, nz)
+    pick = jnp.asarray(np.repeat(np.eye(channels, dtype=np.float32), ROWS, 0).astype(jnp.bfloat16))
+    bias = point_bias.reshape(1, channels)
+    spec = field_spec(channels, nz)
+    mixed_spec = pl.BlockSpec((None,) + grid_modes.shape[1:], lambda x, y: (x, 0, 0))
+    return pl.pallas_call(
+        functools.partial(middle_packed_kernel, devices),
+        grid=(width, ny // STEP),
+        out_shape=(
+            jax.ShapeDtypeStruct(field.shape, jnp.bfloat16),
+            jax.ShapeDtypeStruct((devices * channels, 4 * MZ), jnp.float32),
+            jax.ShapeDtypeStruct((channels // 2, 1, 4 * MZ), jnp.float32),
+        ),
+        in_specs=[mixed_spec, spec, spec, whole(point_weights), whole(bias), whole(pick)]
+        + [whole(t) for t in tables],
+        out_specs=(
+            spec,
+            pl.BlockSpec((devices * channels, 4 * MZ), lambda x, y: (0, 0)),
+            pl.BlockSpec((channels // 2, 1, 4 * MZ), lambda x, y: (0, 0, 0)),
+        ),
+        scratch_shapes=[
+            pltpu.VMEM((channels, ny, 4 * MZ), jnp.float32),
+            pltpu.VMEM((2, ny, channels * MZ), jnp.float32),
+            pltpu.VMEM((channels // 4 * STEP, 4 * nz), jnp.float32),
+            pltpu.VMEM((size, size), jnp.bfloat16),
+            pltpu.VMEM((size, size), jnp.bfloat16),
+            pltpu.VMEM((size, size), jnp.float32),
+            pltpu.VMEM((size, nz), jnp.float32),
+            pltpu.VMEM((channels, 4 * MZ), jnp.float32),
+        ],
+        name="middle_packed",
+    )(grid_modes, field, cotangent, point_weights, bias, pick, *tables)
+
+
+def tail_kernel(
+    devices, channels, scale, src, point_ref, slope_ref, turned_ref, sums_ref, bias_ref,
+    recv, partial, total, gathered, sems, point_sems,
+):
+    me = lax.axis_index("space")
+    greet_peers(devices)
+    meet_peers(devices)
+
+    def point_message(step, phase, source, target):
+        peer = lax.rem(me + step, devices)
+        return pltpu.make_async_remote_copy(
+            src_ref=source(peer),
+            dst_ref=target,
+            send_sem=point_sems.at[phase, 0, step],
+            recv_sem=point_sems.at[phase, 1, step],
+            device_id={"space": peer},
+            device_id_type=pl.DeviceIdType.MESH,
+        )
+
+    def scatter(step, owner):
+        return point_message(step, 0, lambda peer: point_ref.at[peer], partial.at[owner])
+
+    def gather(step, owner):
+        return point_message(step, 1, lambda peer: total, gathered.at[owner])
+
+    def start(make):
+        def one(step, carry):
+            make(step, me).start()
+            return carry
+
+        lax.fori_loop(1, devices, one, 0)
+
+    def finish(make):
+        def one(step, carry):
+            done = make(step, lax.rem(me + devices - step, devices))
+            done.wait_send()
+            done.wait_recv()
+            return carry
+
+        lax.fori_loop(1, devices, one, 0)
+
+    start(scatter)
+    for part in range(channels // 8):
+        send_part(devices, channels, src, recv, sems, part)
+    keep_own(channels, src, recv)
+    partial[me] = point_ref[me]
+    finish(scatter)
+    summed = partial[0]
+    for d in range(1, devices):
+        summed = summed + partial[d]
+    total[...] = summed * scale
+    start(gather)
+    gathered[me] = total[...]
+    weight = jnp.where(lane_ids(8) % MZ == 0, scale, 2.0 * scale)
+
+    def one_part(part, carry):
+        take_part(devices, channels, src, recv, sems, part)
+        first = pl.multiple_of(part * 8, 8)
+        rows = pl.ds(first, 8)
+        parts = [recv[pl.ds(x * channels + first, 8), :] for x in range(devices)]
+        for k, value in enumerate(along_x(parts, 1)):
+            value = value * weight
+            real, imag = value[:, : 2 * MZ], value[:, 2 * MZ :]
+            for alias in range(k, slope_ref.shape[1], devices):
+                slope_ref[0, alias, rows, :] = real
+                slope_ref[1, alias, rows, :] = imag
+                turned_ref[0, alias, rows, :] = imag
+                turned_ref[1, alias, rows, :] = -real
+        return carry
+
+    lax.fori_loop(0, channels // 8, one_part, 0)
+    finish(gather)
+    for d in range(devices):
+        row = gathered[d]
+        both = jnp.concatenate([row[:, : 2 * MZ], row[:, 2 * MZ :]], axis=0)
+        sums_ref[2 * d : 2 * d + 2, :] = both[:, :channels]
+        bias_ref[2 * d : 2 * d + 2, :] = both[:, channels : channels + 1]
+
+
+def tail(modes, point, devices, scale):
+    channels = modes.shape[0] // devices
+    parts = channels // 8
+    vmem = pl.BlockSpec(memory_space=pltpu.VMEM)
+    slope = jax.ShapeDtypeStruct((2, MX, channels, 2 * MZ), jnp.float32)
+    return pl.pallas_call(
+        functools.partial(tail_kernel, devices, channels, scale),
+        out_shape=(
+            slope,
+            slope,
+            jax.ShapeDtypeStruct((channels, channels), jnp.float32),
+            jax.ShapeDtypeStruct((channels, 1), jnp.float32),
+        ),
+        in_specs=[vmem] * 2,
+        out_specs=(vmem,) * 4,
+        scratch_shapes=[
+            pltpu.VMEM((devices * channels, 4 * MZ), jnp.float32),
+            pltpu.VMEM((devices, 1, 4 * MZ), jnp.float32),
+            pltpu.VMEM((1, 4 * MZ), jnp.float32),
+            pltpu.VMEM((devices, 1, 4 * MZ), jnp.float32),
+            pltpu.SemaphoreType.DMA((2, parts, devices)),
+            pltpu.SemaphoreType.DMA((2, 2, devices)),
+        ],
+        compiler_params=pltpu.CompilerParams(collective_id=2, has_side_effects=True, vmem_limit_bytes=8 * 2**20),
+        name="tail",
+    )(modes, point)
 
 
 def x_table(length_x):
@@ -643,12 +895,21 @@
     channels, width, ny, nz = lifted_field.shape
     length_x = width * devices
     scale = 1.0 / float(length_x * ny * nz) ** 0.5
-    packed = width == 1 and MY == 2 * devices and MX % devices == 0 and channels % 8 == 0
+    packed = width == 1 and MY == 2 * devices == channels and MX % devices == 0
     if packed:
         real, imag = front(lifted_field, devices, scale)
         grid_modes = mix_to_grid(real, imag, spectral_weights, devices)[None]
-        local_rows = None
-        spectrum = jnp.stack([real, imag], axis=0)
+        activated, modes, point = middle_packed(
+            grid_modes, devices, lifted_field, cotangent, point_weights, point_bias, scale
+        )
+        slope, turned, summed_point, summed_bias = tail(modes, point, devices, scale)
+        grad_spectral = real[None, :, :, None] * slope[:, :, None] + imag[None, :, :, None] * turned[:, :, None]
+        return (
+            activated,
+            grad_spectral.transpose(0, 1, 4, 2, 3),
+            summed_point,
+            summed_bias.reshape(-1),
+        )
     else:
         spectrum, _ = to_spectrum(forward_modes(lifted_field), scale, devices)
         grid_modes, local_rows = to_grid(mix_modes(spectrum, spectral_weights), length_x)

time: 102 us -> 93.1 us (0.913)
  local copies, waits for them, and re-layouts: 26.5 us -> 15.6 us
  Pallas kernels: 60.7 us -> 64.3 us
    reshape x7 -> x0, local copies, waits for them, and re-layouts: 3.27 us -> none  [the longest x2 1.78 us: to_spectrum(): lines = modes.reshape(width, channels, MY, 2, MZ).transpose(0, 3, 1, 2, 4)]
    pallas_call x2, Pallas kernels: 28.9 us -> 31.4 us  [the longest x1 18.8 us: middle_packed(): pl.pallas_call(functools.partial(middle_packed_kernel, devices), grid=(wi...]
    pallas_call x1, Pallas kernels: 14.3 us -> 16.7 us  [front(): pl.pallas_call(functools.partial(front_kernel, devices, channels, scale),...]
    unnamed x17, local copies, waits for them, and re-layouts: 17.6 us -> 15.6 us
    mul x3 -> x0, local copies, waits for them, and re-layouts: 1.9 us -> none  [the longest x2 1.22 us: weight_gradient(): out = real * slope_modes[:, :, None] + imag * turned[:, :, None]]
    broadcast_in_dim x1 -> x0, local copies, waits for them, and re-layouts: 1.37 us -> none  [middle(): bias = jnp.broadcast_to(point_bias[:, None, None], (channels, 1, nz))]
    pallas_call x1, Pallas kernels: 17.4 us -> 16.1 us  [mix_to_grid(): pl.pallas_call(functools.partial(mix_kernel, devices, channels), out_shap...]
    slice x2 -> x0, local copies, waits for them, and re-layouts: 1.25 us -> none  [the longest x1 1.23 us: body(): local_bias = jnp.sum(slope_modes[:, :, 0, 0], axis=0)]
where the time goes in v2:
time: 93.1 us; the launch traced here: 92.7 us
  Pallas kernels  64.3 us (69%)
  local copies, waits for them, and re-layouts  15.6 us (17%)
  other arithmetic  12.2 us (13%)
    pallas_call x1, Pallas kernels, middle_packed(): pl.pallas_call(functools.partial(middle_packed_kernel, devices), grid=(wi...  18.8 us
    pallas_call x1, Pallas kernels, front(): pl.pallas_call(functools.partial(front_kernel, devices, channels, scale),...  16.7 us
    pallas_call x1, Pallas kernels, mix_to_grid(): pl.pallas_call(functools.partial(mix_kernel, devices, channels), out_shap...  16.1 us
    unnamed x17, local copies, waits for them, and re-layouts  15.6 us
    pallas_call x1, Pallas kernels, tail(): pl.pallas_call(functools.partial(tail_kernel, devices, channels, scale),...  12.6 us
    add x1, other arithmetic, body(): real[None, :, :, None] * slope[:, :, None]  11.6 us

profile of v2, /device:TPU:0, one launch (start us, length us, event | category | flops | bytes accessed | tf_op | source)
XLA Modules:
  0.0 92.7 jit_solution(18081353096088116808)
XLA Ops:
  0.6 16.7 %front.1 = (f32[32,32,64]{2,1,0:T(8,128)}, f32[32,32,64]{2,1,0:T(8,128)}) custom-call(f32[32,1,128,256]{3,2,1,0:T(8,128)} %x_ref.3, bf16[256,128]{1,0:T(8,128)(2,1)} %constant.18.clone.tzh, bf16[256,128]{1,0:T(8,128)(2,1)} %constant.19.clone.tzl, bf16[64,128]{1,0:T(8,128)(2,1)} %constant.20.clone.tyh, bf16[64,128]{1,0:T(8,128)(2,1)} %constant.21.clone.tyl), custom_call_target="tpu_custom_call" | custom-call | tf_op jit(solution)/shard_map/front/pallas_call | solution.py:423
  17.3 0.0 copy-start
  17.3 10.5 %copy-done = f32[2,32,64,32,32]{2,4,3,1,0:T(8,128)S(1)} copy-done((f32[2,32,64,32,32]{2,4,3,1,0:T(8,128)S(1)}, f32[2,32,64,32,32]{2,4,3,1,0:T(8,128)}, u32[]{:S(2)}) %copy-start) | copy-done | bytes 16777240
  27.9 0.0 copy-start.1
  27.9 1.0 %copy-done.1 = f32[32,32,64]{2,1,0:T(8,128)S(1)} copy-done((f32[32,32,64]{2,1,0:T(8,128)S(1)}, f32[32,32,64]{2,1,0:T(8,128)}, u32[]{:S(2)}) %copy-start.1) | copy-done | bytes 262168
  28.9 0.0 copy-start.3
  28.9 1.0 %copy-done.3 = f32[32,32,64]{2,1,0:T(8,128)S(1)} copy-done((f32[32,32,64]{2,1,0:T(8,128)S(1)}, f32[32,32,64]{2,1,0:T(8,128)}, u32[]{:S(2)}) %copy-start.3) | copy-done | bytes 262168
  29.9 0.0 copy-start.2
  29.9 0.0 copy-start.4
  30.0 16.1 %mix.1 = f32[64,1024]{1,0:T(8,128)S(1)} custom-call(f32[32,32,64]{2,1,0:T(8,128)S(1)} %copy-done.1, f32[32,32,64]{2,1,0:T(8,128)S(1)} %copy-done.3, f32[2,32,32,32,64]{4,3,2,1,0:T(8,128)S(1)} %bitcast.7), custom_call_target="tpu_custom_call" | custom-call | tf_op jit(solution)/shard_map/mix/pallas_call | solution.py:501
  46.1 0.0 copy-start.5
  46.1 0.7 copy-done.5
  46.8 18.8 %middle_packed.1 = (bf16[32,1,128,256]{3,2,1,0:T(8,128)(2,1)}, f32[512,128]{1,0:T(8,128)}, f32[16,1,128]{2,1,0:T(1,128)}) custom-call(f32[1,64,1024]{2,1,0:T(8,128)} %bitcast.10, f32[32,1,128,256]{3,2,1,0:T(8,128)} %x_ref.3, bf16[32,1,128,256]{3,2,1,0:T(8,128)(2,1)} %cot_ref.1, f32[32,32]{1,0:T(8,128)} %w_ref.1, f32[1,32]{1,0:T(1,128)} %bitcast.13, ...), custom_call_target="tpu_custom_call" | custom-call | tf_op jit(solution)/shard_map/middle_packed/pallas_call | solution.py:639
  65.6 0.0 copy-start.6
  65.6 0.9 %copy-done.6 = f32[512,128]{1,0:T(8,128)S(1)} copy-done((f32[512,128]{1,0:T(8,128)S(1)}, f32[512,128]{1,0:T(8,128)}, u32[]{:S(2)}) %copy-start.6) | copy-done | bytes 262168
  66.6 0.0 copy-start.7
  66.6 0.7 copy-done.7
  67.3 12.6 %tail.1 = (f32[2,32,32,64]{3,2,1,0:T(8,128)S(1)}, f32[2,32,32,64]{3,2,1,0:T(8,128)S(1)}, f32[32,32]{1,0:T(8,128)S(1)}, f32[32,1]{1,0:T(8,128)S(1)}) custom-call(f32[512,128]{1,0:T(8,128)S(1)} %copy-done.6, f32[16,1,128]{2,1,0:T(1,128)S(1)} %copy-done.7), custom_call_target="tpu_custom_call" | custom-call | tf_op jit(solution)/shard_map/tail/pallas_call | solution.py:752
  79.9 0.6 reduce
  80.5 0.0 copy-done.2
  80.5 0.0 copy-done.4
  80.5 11.6 %multiply_add_fusion = f32[2,32,64,32,32]{2,4,3,1,0:T(8,128)} fusion(f32[2,32,64,32]{2,3,1,0:T(8,128)S(1)} %bitcast.12, f32[32,64,32]{1,2,0:T(8,128)S(1)} %bitcast.9, f32[2,32,64,32]{2,3,1,0:T(8,128)S(1)} %bitcast.11, f32[32,64,32]{1,2,0:T(8,128)S(1)} %bitcast.8), kind=kLoop, calls=%fused_computation | loop fusion | flops 12582912 | bytes 18350080 | tf_op jit(solution)/shard_map/add | solution.py:906
  92.1 0.6 copy.23
Async XLA Ops:
  17.3 10.5 %copy-start = (f32[2,32,64,32,32]{2,4,3,1,0:T(8,128)S(1)}, f32[2,32,64,32,32]{2,4,3,1,0:T(8,128)}, u32[]{:S(2)}) copy-start(f32[2,32,64,32,32]{2,4,3,1,0:T(8,128)} %param.20) | copy-start | bytes 50331652
  27.9 1.0 %copy-start.1 = (f32[32,32,64]{2,1,0:T(8,128)S(1)}, f32[32,32,64]{2,1,0:T(8,128)}, u32[]{:S(2)}) copy-start(f32[32,32,64]{2,1,0:T(8,128)} %get-tuple-element.13.real_ref) | copy-start | bytes 786436
  28.9 1.0 %copy-start.3 = (f32[32,32,64]{2,1,0:T(8,128)S(1)}, f32[32,32,64]{2,1,0:T(8,128)}, u32[]{:S(2)}) copy-start(f32[32,32,64]{2,1,0:T(8,128)} %get-tuple-element.14.imag_ref) | copy-start | bytes 786436
  29.9 50.6 %copy-start.2 = (f32[32,32,64]{2,1,0:T(8,128)S(1)}, f32[32,32,64]{2,1,0:T(8,128)}, u32[]{:S(2)}) copy-start(f32[32,32,64]{2,1,0:T(8,128)} %get-tuple-element.13.real_ref) | copy-start | bytes 786436
  29.9 50.6 %copy-start.4 = (f32[32,32,64]{2,1,0:T(8,128)S(1)}, f32[32,32,64]{2,1,0:T(8,128)}, u32[]{:S(2)}) copy-start(f32[32,32,64]{2,1,0:T(8,128)} %get-tuple-element.14.imag_ref) | copy-start | bytes 786436
  46.1 0.7 copy-start.5
  65.6 1.0 %copy-start.6 = (f32[512,128]{1,0:T(8,128)S(1)}, f32[512,128]{1,0:T(8,128)}, u32[]{:S(2)}) copy-start(f32[512,128]{1,0:T(8,128)} %get-tuple-element.16.src) | copy-start | bytes 786436
  66.6 0.7 copy-start.7

commit v3 on v2

--- a/solution.py
+++ b/solution.py
@@ -415,6 +415,10 @@
         lax.fori_loop(0, channels // 8, finish, 0)
 
 
+def in_hbm(*arrays):
+    return [pltpu.with_memory_space_constraint(a, pltpu.HBM) for a in arrays]
+
+
 def front(field, devices, scale):
     channels, _, ny, nz = field.shape
     tables = packed_tables(ny, nz)
@@ -434,47 +438,59 @@
             pltpu.SemaphoreType.DMA((2, parts, devices)),
         ],
         compiler_params=pltpu.CompilerParams(
-            collective_id=0, has_side_effects=True
+            collective_id=0, has_side_effects=True, vmem_limit_bytes=20 * 2**20
         ),
         name="front",
-    )(field, *tables)
-
-
-def mix_kernel(devices, channels, real_ref, imag_ref, w_ref, out_ref, mixed, src, recv, sems):
+    )(*in_hbm(field, *tables))
+
+
+def mix_kernel(devices, channels, real_ref, imag_ref, w_ref, out_ref, both, mixed, src, recv, sems):
     greet_peers(devices)
     local = real_ref.shape[2]
     aliases = range(0, real_ref.shape[0], devices)
     parts = channels // 8
-
-    def one_k(k, carry):
-        totals = [jnp.zeros((8, local), jnp.float32)] * (2 * parts)
-        for i in range(channels):
-            real = jnp.broadcast_to(real_ref[k, i : i + 1, :], (8, local))
-            imag = jnp.broadcast_to(imag_ref[k, i : i + 1, :], (8, local))
-            for part in range(parts):
-                rows = slice(part * 8, part * 8 + 8)
-                w_real = w_ref[0, k, i, rows, :]
-                w_imag = w_ref[1, k, i, rows, :]
-                for alias in aliases[1:]:
-                    w_real = w_real + w_ref[0, k + alias, i, rows, :]
-                    w_imag = w_imag + w_ref[1, k + alias, i, rows, :]
-                totals[2 * part] = totals[2 * part] + (real * w_real - imag * w_imag)
-                totals[2 * part + 1] = totals[2 * part + 1] + (real * w_imag + imag * w_real)
-        for part in range(parts):
-            mixed[k, part] = jnp.concatenate(totals[2 * part : 2 * part + 2], axis=1)
+    for k in range(devices):
+        both[0, k] = jnp.concatenate([real_ref[k]] * 2, axis=1)
+        both[1, k] = jnp.concatenate([imag_ref[k]] * 2, axis=1)
+
+    def one_half(half, carry):
+        def one_k(k, inner):
+            by_real = [jnp.zeros((8, 2 * local), jnp.float32)] * 2
+            by_imag = [jnp.zeros((8, 2 * local), jnp.float32)] * 2
+            for i in range(channels):
+                real = jnp.broadcast_to(both[0, k, i : i + 1, :], (8, 2 * local))
+                imag = jnp.broadcast_to(both[1, k, i : i + 1, :], (8, 2 * local))
+                for part in range(2):
+                    rows = pl.ds(pl.multiple_of(half * 16 + part * 8, 8), 8)
+                    w_real = w_ref[0, k, i, rows, :]
+                    w_imag = w_ref[1, k, i, rows, :]
+                    for alias in aliases[1:]:
+                        w_real = w_real + w_ref[0, k + alias, i, rows, :]
+                        w_imag = w_imag + w_ref[1, k + alias, i, rows, :]
+                    pair = jnp.concatenate([w_real, w_imag], axis=1)
+                    by_real[part] = by_real[part] + real * pair
+                    by_imag[part] = by_imag[part] + imag * pair
+            for part in range(2):
+                mixed[k, part] = by_real[part] - turn(by_imag[part])
+            return inner
+
+        lax.fori_loop(0, devices, one_k, 0)
+
+        @pl.when(half == 0)
+        def _():
+            meet_peers(devices)
+
+        def one_part(part, inner):
+            start = pl.multiple_of(half * 16 + part * 8, 8)
+            for x, value in enumerate(along_x([mixed[k, part] for k in range(devices)], -1)):
+                src[pl.ds(x * channels + start, 8), :] = value
+            send_part(devices, channels, src, recv, sems, half * 2 + part)
+            return inner
+
+        lax.fori_loop(0, 2, one_part, 0)
         return carry
 
-    lax.fori_loop(0, devices, one_k, 0)
-    meet_peers(devices)
-
-    def one_part(part, carry):
-        start = pl.multiple_of(part * 8, 8)
-        for x, value in enumerate(along_x([mixed[k, part] for k in range(devices)], -1)):
-            src[pl.ds(x * channels + start, 8), :] = value
-        send_part(devices, channels, src, recv, sems, part)
-        return carry
-
-    lax.fori_loop(0, parts, one_part, 0)
+    lax.fori_loop(0, parts // 2, one_half, 0)
     keep_own(channels, src, recv)
 
     def finish(part, carry):
@@ -504,7 +520,8 @@
         in_specs=[vmem, vmem, vmem],
         out_specs=vmem,
         scratch_shapes=[
-            pltpu.VMEM((devices, channels // 8, 8, 4 * MZ), jnp.float32),
+            pltpu.VMEM((2, devices, channels, 4 * MZ), jnp.float32),
+            pltpu.VMEM((devices, 2, 8, 4 * MZ), jnp.float32),
             pltpu.VMEM((devices * channels, 4 * MZ), jnp.float32),
             pltpu.VMEM((devices * channels, 4 * MZ), jnp.float32),
             pltpu.SemaphoreType.DMA((2, channels // 8, devices)),
@@ -661,8 +678,9 @@
             pltpu.VMEM((size, nz), jnp.float32),
             pltpu.VMEM((channels, 4 * MZ), jnp.float32),
         ],
+        compiler_params=pltpu.CompilerParams(vmem_limit_bytes=28 * 2**20),
         name="middle_packed",
-    )(grid_modes, field, cotangent, point_weights, bias, pick, *tables)
+    )(grid_modes, *in_hbm(field, cotangent, point_weights, bias, pick, *tables))
 
 
 def tail_kernel(

time: 93.1 us -> 86.7 us (0.931)
  local copies, waits for them, and re-layouts: 15.6 us -> 11.1 us
  Pallas kernels: 64.3 us -> 62.5 us
    unnamed x17 -> x3, local copies, waits for them, and re-layouts: 15.6 us -> 11.1 us
    pallas_call x1, Pallas kernels: 16.7 us -> 15.7 us  [front(): pl.pallas_call(functools.partial(front_kernel, devices, channels, scale),...]
where the time goes in v3:
time: 86.7 us; the launch traced here: 86.5 us
  Pallas kernels  62.5 us (72%)
  other arithmetic  12.2 us (14%)
  local copies, waits for them, and re-layouts  11.1 us (13%)
    pallas_call x1, Pallas kernels, middle_packed(): pl.pallas_call(functools.partial(middle_packed_kernel, devices), grid=(wi...  18.6 us
    pallas_call x1, Pallas kernels, front(): pl.pallas_call(functools.partial(front_kernel, devices, channels, scale),...  15.7 us
    pallas_call x1, Pallas kernels, mix_to_grid(): pl.pallas_call(functools.partial(mix_kernel, devices, channels), out_shap...  15.4 us
    pallas_call x1, Pallas kernels, tail(): pl.pallas_call(functools.partial(tail_kernel, devices, channels, scale),...  12.8 us
    add x1, other arithmetic, body(): real[None, :, :, None] * slope[:, :, None]  11.6 us
    unnamed x3, local copies, waits for them, and re-layouts  11.1 us

profile of v3, /device:TPU:0, one launch (start us, length us, event | category | flops | bytes accessed | tf_op | source)
XLA Modules:
  0.0 86.5 jit_solution(12125798060356841673)
XLA Ops:
  0.6 15.7 %front.1 = (f32[32,32,64]{2,1,0:T(8,128)S(1)}, f32[32,32,64]{2,1,0:T(8,128)S(1)}) custom-call(f32[32,1,128,256]{3,2,1,0:T(8,128)} %x_ref.3, bf16[256,128]{1,0:T(8,128)(2,1)} %constant.18.clone.tzh, bf16[256,128]{1,0:T(8,128)(2,1)} %constant.19.clone.tzl, bf16[64,128]{1,0:T(8,128)(2,1)} %constant.20.clone.tyh, bf16[64,128]{1,0:T(8,128)(2,1)} %constant.21.clone.tyl), custom_call_target="tpu_custom_call" | custom-call | tf_op jit(solution)/shard_map/front/pallas_call | solution.py:427
  16.4 0.0 copy-start
  16.4 10.5 %copy-done = f32[2,32,64,32,32]{2,4,3,1,0:T(8,128)S(1)} copy-done((f32[2,32,64,32,32]{2,4,3,1,0:T(8,128)S(1)}, f32[2,32,64,32,32]{2,4,3,1,0:T(8,128)}, u32[]{:S(2)}) %copy-start) | copy-done | bytes 16777240
  26.9 15.4 %mix.1 = f32[64,1024]{1,0:T(8,128)S(1)} custom-call(f32[32,32,64]{2,1,0:T(8,128)S(1)} %get-tuple-element.13.real_ref, f32[32,32,64]{2,1,0:T(8,128)S(1)} %get-tuple-element.14.imag_ref, f32[2,32,32,32,64]{4,3,2,1,0:T(8,128)S(1)} %bitcast.7), custom_call_target="tpu_custom_call" | custom-call | tf_op jit(solution)/shard_map/mix/pallas_call | solution.py:517
  42.3 18.6 %middle_packed.1 = (bf16[32,1,128,256]{3,2,1,0:T(8,128)(2,1)}, f32[512,128]{1,0:T(8,128)S(1)}, f32[16,1,128]{2,1,0:T(1,128)S(1)}) custom-call(f32[1,64,1024]{2,1,0:T(8,128)S(1)} %bitcast.10, f32[32,1,128,256]{3,2,1,0:T(8,128)} %x_ref.3, bf16[32,1,128,256]{3,2,1,0:T(8,128)(2,1)} %cot_ref.1, f32[32,32]{1,0:T(8,128)} %w_ref.1, f32[1,32]{1,0:T(1,128)} %bitcast.13, ...), custom_call_target="tpu_custom_call" | custom-call | tf_op jit(solution)/shard_map/middle_packed/pallas_call | solution.py:656
  61.0 12.8 %tail.1 = (f32[2,32,32,64]{3,2,1,0:T(8,128)S(1)}, f32[2,32,32,64]{3,2,1,0:T(8,128)S(1)}, f32[32,32]{1,0:T(8,128)S(1)}, f32[32,1]{1,0:T(8,128)S(1)}) custom-call(f32[512,128]{1,0:T(8,128)S(1)} %get-tuple-element.16.src, f32[16,1,128]{2,1,0:T(1,128)S(1)} %get-tuple-element.17.point_ref), custom_call_target="tpu_custom_call" | custom-call | tf_op jit(solution)/shard_map/tail/pallas_call | solution.py:770
  73.7 0.6 reduce
  74.3 11.6 %multiply_add_fusion = f32[2,32,64,32,32]{2,4,3,1,0:T(8,128)} fusion(f32[2,32,64,32]{2,3,1,0:T(8,128)S(1)} %bitcast.12, f32[32,64,32]{1,2,0:T(8,128)S(1)} %bitcast.9, f32[2,32,64,32]{2,3,1,0:T(8,128)S(1)} %bitcast.11, f32[32,64,32]{1,2,0:T(8,128)S(1)} %bitcast.8), kind=kLoop, calls=%fused_computation | loop fusion | flops 12582912 | bytes 18350080 | tf_op jit(solution)/shard_map/add | solution.py:924
  85.9 0.6 copy.23
Async XLA Ops:
  16.4 10.5 %copy-start = (f32[2,32,64,32,32]{2,4,3,1,0:T(8,128)S(1)}, f32[2,32,64,32,32]{2,4,3,1,0:T(8,128)}, u32[]{:S(2)}) copy-start(f32[2,32,64,32,32]{2,4,3,1,0:T(8,128)} %param.20) | copy-start | bytes 50331652
